TPU v7x, 256 devices: a whole 4x4x8 slice. The times are simulated.
256 devices in a mesh: fsdp: 8 (over z_hi, y), tensor: 32 (over x, z_lo, core).
Axes of the slice: x: 4, y: 4, z: 8 (z_hi: 2, z_lo: 4; z = z_hi * 4 + z_lo), core: 2. Of those that a mesh axis runs over, the one named last changes fastest.
Arguments:
- momentum: bfloat16 [8192, 28672], P('fsdp', 'tensor'), may hold values from -6 to 6
- gradient: bfloat16 [8192, 28672], P('fsdp', 'tensor'), may hold values from -4 to 4
- factor: float32 [28672, 512], P('tensor', 'fsdp'), may hold values from -0.03125 to 0.03125
Outputs:
- new_momentum: bfloat16 [8192, 28672], P('fsdp', 'tensor')
- new_factor: float32 [28672, 512], P('tensor', 'fsdp')
- update: bfloat16 [8192, 28672], P('fsdp', 'tensor')
All inputs are finite; a program needn't handle non-finite values.
Results may differ from a plain program's by a relative error of at most 0.017.
Values may be sent and summed in bfloat16 or wider, within the bound.
No kernel may reach another device: no remote copies, remote signals or barrier semaphores. Data moves between devices by JAX's collectives and lax.ppermute only.
A program may use at most 64 MiB of HBM per device.

v0:
```python
import jax
import jax.numpy as jnp
from jax import lax
from jax.sharding import Mesh
from jax.sharding import PartitionSpec as P

D = 8192
FF = 28672
R = 512
TENSOR = ("tensor_0", "tensor_1", "tensor_2")
decay_rate = 0.95
epsilon = 1e-06


def from_everyone(value, axis):
    length = lax.axis_size(axis)
    return lax.all_to_all(
        jnp.broadcast_to(value[None], (length, *value.shape)), axis, 0, 0, tiled=True
    )


def laid_out(pieces, dim):
    lengths = list(pieces.shape[1:])
    lengths[dim] *= pieces.shape[0]
    return jnp.moveaxis(pieces, 0, dim).reshape(lengths)


def collect(value, axis, dim):
    pieces = from_everyone(value, axis)
    return laid_out(pieces, dim)


def padded_to(lines, length):
    spare = -lines.shape[0] % length
    if not spare:
        return lines
    return jnp.concatenate([lines, jnp.zeros((spare, *lines.shape[1:]), lines.dtype)])


def gather_axes(value, axes, dim):
    far, near = axes
    leading = from_everyone(value, far)
    pieces = jnp.swapaxes(from_everyone(leading, near), 0, 1)
    return laid_out(pieces.reshape(-1, *value.shape), dim)


def in_blocks(value, dim, length):
    before, after = (value.shape[:dim], value.shape[dim + 1 :])
    return jnp.moveaxis(value.reshape(*before, length, -1, *after), dim, 0)


def sum_at_owner(value, axis, dim):
    length = lax.axis_size(axis)
    pieces = lax.all_to_all(in_blocks(value, dim, length), axis, 0, 0, tiled=True)
    return jnp.sum(pieces, axis=0)


def sum_by_axis(value, axes, dim):
    far, near = axes
    pieces = in_blocks(value, dim, lax.axis_size(far))
    nearer = sum_at_owner(pieces, near, dim + 1)
    arrived = lax.all_to_all(nearer, far, split_axis=0, concat_axis=0, tiled=True)
    return arrived.sum(axis=0)


def sum_by_parts(value, axes):
    lines = value.reshape(-1, value.shape[-1])
    padded = padded_to(lines, lax.axis_size(axes[0]) * lax.axis_size(axes[1]))
    whole = gather_axes(sum_by_axis(padded, axes, 0), axes, 0)
    return lax.slice_in_dim(whole, 0, len(lines)).reshape(value.shape)


def over_copies(value, axis):
    everything = from_everyone(value, axis)
    return jnp.sum(everything, axis=0)


def on_device(momentum, gradient, factor):
    blended = (momentum.astype(jnp.float32) + gradient.astype(jnp.float32)).astype(jnp.bfloat16)
    lowered = factor.astype(jnp.bfloat16)
    columns = factor.shape[1]
    partial_left = jnp.dot(blended, collect(lowered, "fsdp", 1), preferred_element_type=jnp.float32)
    left_factor = sum_by_parts(partial_left, (("tensor_0", "tensor_1"), "tensor_2"))
    local_gram = lax.dot_general(
        left_factor, left_factor, (((0,), (0,)), ((), ())), precision=lax.Precision.HIGHEST
    )
    gram_matrix = lax.psum(local_gram, "fsdp")
    lower_factor = jnp.linalg.cholesky(gram_matrix)
    solved = jax.scipy.linalg.solve_triangular(lower_factor, left_factor.T, lower=True)
    orthonormal = solved.T.astype(jnp.bfloat16)
    partial_right = lax.dot_general(
        blended, orthonormal, (((0,), (0,)), ((), ())), preferred_element_type=jnp.float32
    )
    right_factor = lax.psum(partial_right.astype(jnp.bfloat16), "fsdp").astype(jnp.float32)
    square_sums = over_copies(jnp.sum(right_factor * right_factor, axis=0), TENSOR)
    inverse = lax.rsqrt(square_sums + epsilon)
    full_factor = right_factor * inverse[None, :]
    own_factor = lax.dynamic_slice_in_dim(full_factor, lax.axis_index("fsdp") * columns, columns, 1)
    product = lax.dot_general(
        orthonormal,
        right_factor.astype(jnp.bfloat16),
        (((1,), (1,)), ((), ())),
        preferred_element_type=jnp.float32,
    )
    stepped = lax.dot_general(
        orthonormal,
        full_factor.astype(jnp.bfloat16),
        (((1,), (1,)), ((), ())),
        preferred_element_type=jnp.float32,
    )
    new_momentum = (blended.astype(jnp.float32) - (1.0 - decay_rate) * product).astype(jnp.bfloat16)
    update = (stepped * jnp.sqrt(jnp.float32(D * FF / R))).astype(jnp.bfloat16)
    return (new_momentum, own_factor, update)


def solution(mesh):
    torus = Mesh(
        mesh.devices.reshape(mesh.shape["fsdp"], 4, 4, 2),
        ("fsdp", "tensor_0", "tensor_1", "tensor_2"),
    )
    return jax.shard_map(
        on_device,
        mesh=torus,
        in_specs=(P("fsdp", TENSOR), P("fsdp", TENSOR), P(TENSOR, "fsdp")),
        out_specs=(P("fsdp", TENSOR), P(TENSOR, "fsdp"), P("fsdp", TENSOR)),
        check_vma=False,
    )
```

profile of v0, /device:TPU:1, one launch (start us, length us, event | category | flops | bytes accessed | tf_op | source)
XLA Modules:
  0.0 529.0 jit_solution(15417045091283632723)
XLA Ops:
  9.3 11.6 %all-to-all-start = ((bf16[8,896,64]{1,2,0:T(8,128)(2,1)}), bf16[8,896,64]{1,2,0:T(8,128)(2,1)S(1)}, u32[]{:S(2)}, u32[]{:S(2)}) async-start(bf16[8,896,64]{1,2,0:T(8,128)(2,1)} %broadcast_in_dim.9), calls=%async_computation | async-start | bytes 1835008 | tf_op jit(solution)/shard_map/all_to_all | solution.py:17
  21.0 3.2 add_convert_fusion
  24.2 13.0 %all-to-all-done = bf16[8,896,64]{1,2,0:T(8,128)(2,1)S(1)} async-done(((bf16[8,896,64]{1,2,0:T(8,128)(2,1)}), bf16[8,896,64]{1,2,0:T(8,128)(2,1)S(1)}, u32[]{:S(2)}, u32[]{:S(2)}) %all-to-all-start) | async-done | bytes 917536 | tf_op jit(solution)/shard_map/all_to_all | solution.py:17
  40.3 11.2 %all_to_all.31 = f32[2,16,32,512]{3,2,1,0:T(8,128)S(1)} all-to-all(f32[2,16,32,512]{3,2,1,0:T(8,128)S(1)} %copy.29), channel_id=1, replica_groups=mesh['fsdp'=8,'tensor_0'=4,'tensor_1'=4,'tensor_2'=2] {'tensor_2'}, dimensions={0} | all-to-all | bytes 4194304 | tf_op jit(solution)/shard_map/all_to_all | solution.py:54
  51.8 37.0 %all_to_all.32 = f32[16,32,512]{2,1,0:T(8,128)S(1)} all-to-all(f32[16,32,512]{2,1,0:T(8,128)S(1)} %reduce_sum.36), channel_id=1, replica_groups=mesh['fsdp'=8,'tensor_0'=4,'tensor_1'=4,'tensor_2'=2] {'tensor_0','tenso..., dimensions={0} | all-to-all | bytes 2097152 | tf_op jit(solution)/shard_map/all_to_all | solution.py:62
  88.9 30.9 %all_to_all.33 = f32[16,32,512]{2,1,0:T(8,128)S(1)} all-to-all(f32[16,32,512]{2,1,0:T(8,128)S(1)} %broadcast_in_dim.10), channel_id=1, replica_groups=mesh['fsdp'=8,'tensor_0'=4,'tensor_1'=4,'tensor_2'=2] {'tensor_0','tenso..., dimensions={0} | all-to-all | bytes 2097152 | tf_op jit(solution)/shard_map/all_to_all | solution.py:17
  120.1 6.8 %all_to_all.34 = f32[2,16,32,512]{3,2,1,0:T(8,128)S(1)} all-to-all(f32[2,16,32,512]{3,2,1,0:T(8,128)S(1)} %broadcast_in_dim.11), channel_id=1, replica_groups=mesh['fsdp'=8,'tensor_0'=4,'tensor_1'=4,'tensor_2'=2] {'tensor_2'}, dimensions={0} | all-to-all | bytes 4194304 | tf_op jit(solution)/shard_map/all_to_all | solution.py:17
  126.8 4.5 fusion.9
  135.4 97.5 %all-reduce.4.cloned.1.call-done = f32[512,512]{0,1:T(8,128)} async-done(((f32[512,512]{0,1:T(8,128)}), f32[512,512]{0,1:T(8,128)}) %all-reduce.4.cloned.1.call-update) | async-done | bytes 1048592 | tf_op jit(solution)/shard_map/psum | solution.py:87
  238.0 11.7 %cholesky.104 = f32[128,128]{1,0:T(8,128)S(1)} custom-call(f32[128,128]{1,0:T(8,128)S(1)} %cholesky.266), custom_call_target="Cholesky" | custom-call | tf_op jit(solution)/shard_map/jit(cholesky)/cholesky | solution.py:88
  249.8 9.8 %custom-call.31 = f32[1,128,128]{1,2,0:T(8,128)S(1)} custom-call(f32[1,128,128]{2,1,0:T(8,128)S(1)} %get-tuple-element.45), custom_call_target="InvertDiagBlocksLowerTriangular" | custom-call | tf_op jit(solution)/shard_map/jit(cholesky)/cholesky | solution.py:88
  262.2 11.7 %cholesky.217 = f32[128,128]{1,0:T(8,128)S(1)} custom-call(f32[128,128]{1,0:T(8,128)S(1)} %cholesky.270), custom_call_target="Cholesky" | custom-call | tf_op jit(solution)/shard_map/jit(cholesky)/cholesky | solution.py:88
  273.9 10.0 %custom-call.32 = f32[1,128,128]{1,2,0:T(8,128)S(1)} custom-call(f32[1,128,128]{2,1,0:T(8,128)S(1)} %get-tuple-element.42), custom_call_target="InvertDiagBlocksLowerTriangular" | custom-call | tf_op jit(solution)/shard_map/jit(cholesky)/cholesky | solution.py:88
  285.4 11.7 %cholesky.238 = f32[128,128]{1,0:T(8,128)S(1)} custom-call(f32[128,128]{1,0:T(8,128)S(1)} %cholesky.275), custom_call_target="Cholesky" | custom-call | tf_op jit(solution)/shard_map/jit(cholesky)/cholesky | solution.py:88
  297.9 9.8 %custom-call.33 = f32[1,128,128]{1,2,0:T(8,128)S(1)} custom-call(f32[1,128,128]{2,1,0:T(8,128)S(1)} %get-tuple-element.39), custom_call_target="InvertDiagBlocksLowerTriangular" | custom-call | tf_op jit(solution)/shard_map/jit(cholesky)/cholesky | solution.py:88
  309.2 11.7 %cholesky.255 = f32[128,128]{1,0:T(8,128)S(1)} custom-call(f32[128,128]{1,0:T(8,128)S(1)} %convolution_subtract_fusion.4), custom_call_target="Cholesky" | custom-call | tf_op jit(solution)/shard_map/jit(cholesky)/cholesky | solution.py:88
  326.1 14.1 %while.1 = (s32[]{:T(128)}, f32[512,512]{1,0:T(8,128)}, s32[4,2]{0,1:T(2,128)S(1)}, f32[4,128,128]{2,1,0:T(8,128)}, s32[]{:T(128)}) while((s32[]{:T(128)}, f32[512,512]{1,0:T(8,128)}, s32[4,2]{0,1:T(2,128)S(1)}, f32[4,128,128]{2,1,0:T(8,128)}, s32[]{:T(128)}) %tuple.39), condition=%wide.while_cond, body=%wide.while_body.sunk | while | flops 2 | bytes 132705 | solution.py:89
  326.7 2.9 bitcast_dynamic-update-slice_fusion.2
  330.3 2.9 bitcast_dynamic-update-slice_fusion.2
  340.2 40.1 %custom-call.34 = f32[4,128,128]{1,2,0:T(8,128)S(1)} custom-call(f32[4,128,128]{2,1,0:T(8,128)} %get-tuple-element.10), custom_call_target="InvertDiagBlocksLowerTriangular" | custom-call | tf_op jit(solution)/shard_map/jit(_solve_triangular)/triangular_solve | solution.py:89
  390.4 106.7 %all-reduce.6.cloned.1.call-done = bf16[896,512]{1,0:T(8,128)(2,1)} async-done(((bf16[896,512]{1,0:T(8,128)(2,1)}), bf16[896,512]{1,0:T(8,128)(2,1)}) %all-reduce.6.cloned.1.call-update) | async-done | bytes 917520 | tf_op jit(solution)/shard_map/psum | solution.py:94
  499.2 11.0 %all-to-all-start.5 = ((f32[32,1,512]{2,1,0:T(1,128)}), f32[32,1,512]{2,1,0:T(1,128)S(1)}, u32[]{:S(2)}, u32[]{:S(2)}) async-start(f32[32,1,512]{2,1,0:T(1,128)} %broadcast_in_dim.12), calls=%async_computation.5 | async-start | bytes 131072 | tf_op jit(solution)/shard_map/all_to_all | solution.py:17
  510.2 4.0 subtract_convert_fusion
  514.2 3.8 all-to-all-done.5
  (83 shorter events, 48.4 us)
Async XLA Ops:
  7.2 13.8 %copy-start.3 = (bf16[1024,896]{1,0:T(8,128)(2,1)S(1)}, bf16[1024,896]{1,0:T(8,128)(2,1)}, u32[]{:S(2)}) copy-start(bf16[1024,896]{1,0:T(8,128)(2,1)} %param.4) | copy-start | bytes 5505028
  9.3 27.9 %all-to-all-start = ((bf16[8,896,64]{1,2,0:T(8,128)(2,1)}), bf16[8,896,64]{1,2,0:T(8,128)(2,1)S(1)}, u32[]{:S(2)}, u32[]{:S(2)}) async-start(bf16[8,896,64]{1,2,0:T(8,128)(2,1)} %broadcast_in_dim.9), calls=%async_computation | async-start | bytes 1835008 | tf_op jit(solution)/shard_map/all_to_all | solution.py:17
  21.0 211.9 %all-reduce.4.cloned.1.call-start = ((), (), s32[]{:S(2)}) async-start(), calls=%async_computation.6 | async-start | bytes 2097152 | tf_op jit(solution)/shard_map/psum | solution.py:87
  131.4 365.7 %all-reduce.6.cloned.1.call-start = ((), (), s32[]{:S(2)}) async-start(), calls=%async_computation.7 | async-start | bytes 1835008 | tf_op jit(solution)/shard_map/psum | solution.py:94
  232.9 2.6 copy-start
  237.0 1.0 copy-start.2
  383.0 5.2 copy-start.6
  385.4 2.8 copy-start.8
  385.4 2.8 copy-start.4
  388.2 122.0 %copy-start.5 = (bf16[1024,896]{1,0:T(8,128)(2,1)S(1)}, bf16[1024,896]{1,0:T(8,128)(2,1)}, u32[]{:S(2)}) copy-start(bf16[1024,896]{1,0:T(8,128)(2,1)} %add_convert_fusion) | copy-start | bytes 5505028
  499.2 18.8 %all-to-all-start.5 = ((f32[32,1,512]{2,1,0:T(1,128)}), f32[32,1,512]{2,1,0:T(1,128)S(1)}, u32[]{:S(2)}, u32[]{:S(2)}) async-start(f32[32,1,512]{2,1,0:T(1,128)} %broadcast_in_dim.12), calls=%async_computation.5 | async-start | bytes 131072 | tf_op jit(solution)/shard_map/all_to_all | solution.py:17
  510.2 7.9 %copy-start.1 = (bf16[896,512]{1,0:T(8,128)(2,1)S(1)}, bf16[896,512]{1,0:T(8,128)(2,1)}, u32[]{:S(2)}) copy-start(bf16[896,512]{1,0:T(8,128)(2,1)} %all-reduce.6.cloned.1.call-done) | copy-start | bytes 2752516
  518.1 1.3 copy-start.7
  518.1 1.3 copy-start.9
Sparse Core Ops, SparseCore 0:
  131.5 101.3 all-reduce.3
  390.5 106.5 all-reduce.5
where the time goes:
time: 536 us; the launch traced here: 529 us
  waiting for transfers between devices  221 us (41%)
  other arithmetic  128 us (24%)
  blocking collectives  85.8 us (16%)
  matrix products  29.2 us (5%)
  local copies, waits for them, and re-layouts  25.2 us (5%)
  starting transfers between devices  22.7 us (4%)
  between operations  17.2 us (3%)
    psum x1, waiting for transfers between devices, on_device(): lax.psum(partial_right.astype(jnp.bfloat16), 'fsdp').astype(jnp.float32)  107 us
    psum x1, waiting for transfers between devices, on_device(): gram_matrix = lax.psum(local_gram, 'fsdp')  97.5 us
    another operation x14, other arithmetic, on_device(): lower_factor = jnp.linalg.cholesky(gram_matrix)  78.6 us
    another operation x3, other arithmetic, on_device(): jax.scipy.linalg.solve_triangular(lower_factor, left_factor.T, lower=True)  41.4 us
    all_to_all x2, blocking collectives, from_everyone(): lax.all_to_all(jnp.broadcast_to(value[None], (length, *value.shape)), axi...  37.6 us
    all_to_all x1, blocking collectives, sum_by_axis(): lax.all_to_all(nearer, far, split_axis=0, concat_axis=0, tiled=True)  37 us
    all_to_all x2, starting transfers between devices, from_everyone(): lax.all_to_all(jnp.broadcast_to(value[None], (length, *value.shape)), axi...  22.7 us
    all_to_all x2, waiting for transfers between devices, from_everyone(): lax.all_to_all(jnp.broadcast_to(value[None], (length, *value.shape)), axi...  16.8 us
  transfers between devices with their start and end apart: 4, of which 4 were waited for; matrix products, arithmetic and copies ran while one was open for 2% of the time, Pallas kernels for 0%

commit v1 on v0

--- a/solution.py
+++ b/solution.py
@@ -84,7 +84,13 @@
     local_gram = lax.dot_general(
         left_factor, left_factor, (((0,), (0,)), ((), ())), precision=lax.Precision.HIGHEST
     )
-    gram_matrix = lax.psum(local_gram, "fsdp")
+
+    def shape_circles(x_local):
+        part_now = lax.all_gather(x_local, "fsdp")
+        top = jnp.sum(part_now, 0)
+        return top
+
+    gram_matrix = shape_circles(local_gram)
     lower_factor = jnp.linalg.cholesky(gram_matrix)
     solved = jax.scipy.linalg.solve_triangular(lower_factor, left_factor.T, lower=True)
     orthonormal = solved.T.astype(jnp.bfloat16)

time: 536 us -> 599 us (1.12)
  waiting for transfers between devices: 221 us -> 281 us
    all_gather x0 -> x1, waiting for transfers between devices: none -> 163 us  [shape_circles(): part_now = lax.all_gather(x_local, 'fsdp')]
    psum x1 -> x0, waiting for transfers between devices: 97.5 us -> none  [on_device(): gram_matrix = lax.psum(local_gram, 'fsdp')]
where the time goes in v1:
time: 599 us; the launch traced here: 592 us
  waiting for transfers between devices  281 us (47%)
  other arithmetic  132 us (22%)
  blocking collectives  85.8 us (14%)
  matrix products  29.2 us (5%)
  local copies, waits for them, and re-layouts  24 us (4%)
  starting transfers between devices  23.1 us (4%)
  between operations  17.2 us (3%)
    all_gather x1, waiting for transfers between devices, shape_circles(): part_now = lax.all_gather(x_local, 'fsdp')  163 us
    psum x1, waiting for transfers between devices, on_device(): lax.psum(partial_right.astype(jnp.bfloat16), 'fsdp').astype(jnp.float32)  101 us
    another operation x14, other arithmetic, on_device(): lower_factor = jnp.linalg.cholesky(gram_matrix)  78.8 us
    another operation x3, other arithmetic, on_device(): jax.scipy.linalg.solve_triangular(lower_factor, left_factor.T, lower=True)  41.2 us
    all_to_all x2, blocking collectives, from_everyone(): lax.all_to_all(jnp.broadcast_to(value[None], (length, *value.shape)), axi...  37.6 us
    all_to_all x1, blocking collectives, sum_by_axis(): lax.all_to_all(nearer, far, split_axis=0, concat_axis=0, tiled=True)  37 us
    all_to_all x2, starting transfers between devices, from_everyone(): lax.all_to_all(jnp.broadcast_to(value[None], (length, *value.shape)), axi...  23 us
    all_to_all x2, waiting for transfers between devices, from_everyone(): lax.all_to_all(jnp.broadcast_to(value[None], (length, *value.shape)), axi...  16.7 us
  transfers between devices with their start and end apart: 4, of which 4 were waited for; matrix products, arithmetic and copies ran while one was open for 2% of the time, Pallas kernels for 0%

profile of v1, /device:TPU:1, one launch (start us, length us, event | category | flops | bytes accessed | tf_op | source)
XLA Modules:
  0.0 592.4 jit_solution(1439421644321437870)
XLA Ops:
  9.3 11.6 %all-to-all-start = ((bf16[8,896,64]{1,2,0:T(8,128)(2,1)}), bf16[8,896,64]{1,2,0:T(8,128)(2,1)S(1)}, u32[]{:S(2)}, u32[]{:S(2)}) async-start(bf16[8,896,64]{1,2,0:T(8,128)(2,1)} %broadcast_in_dim.9), calls=%async_computation | async-start | bytes 1835008 | tf_op jit(solution)/shard_map/all_to_all | solution.py:17
  21.0 3.2 add_convert_fusion
  24.2 13.0 %all-to-all-done = bf16[8,896,64]{1,2,0:T(8,128)(2,1)S(1)} async-done(((bf16[8,896,64]{1,2,0:T(8,128)(2,1)}), bf16[8,896,64]{1,2,0:T(8,128)(2,1)S(1)}, u32[]{:S(2)}, u32[]{:S(2)}) %all-to-all-start) | async-done | bytes 917536 | tf_op jit(solution)/shard_map/all_to_all | solution.py:17
  40.3 11.2 %all_to_all.31 = f32[2,16,32,512]{3,2,1,0:T(8,128)S(1)} all-to-all(f32[2,16,32,512]{3,2,1,0:T(8,128)S(1)} %copy.25), channel_id=1, replica_groups=mesh['fsdp'=8,'tensor_0'=4,'tensor_1'=4,'tensor_2'=2] {'tensor_2'}, dimensions={0} | all-to-all | bytes 4194304 | tf_op jit(solution)/shard_map/all_to_all | solution.py:54
  51.8 37.0 %all_to_all.32 = f32[16,32,512]{2,1,0:T(8,128)S(1)} all-to-all(f32[16,32,512]{2,1,0:T(8,128)S(1)} %reduce_sum.45), channel_id=1, replica_groups=mesh['fsdp'=8,'tensor_0'=4,'tensor_1'=4,'tensor_2'=2] {'tensor_0','tenso..., dimensions={0} | all-to-all | bytes 2097152 | tf_op jit(solution)/shard_map/all_to_all | solution.py:62
  88.9 30.9 %all_to_all.33 = f32[16,32,512]{2,1,0:T(8,128)S(1)} all-to-all(f32[16,32,512]{2,1,0:T(8,128)S(1)} %broadcast_in_dim.10), channel_id=1, replica_groups=mesh['fsdp'=8,'tensor_0'=4,'tensor_1'=4,'tensor_2'=2] {'tensor_0','tenso..., dimensions={0} | all-to-all | bytes 2097152 | tf_op jit(solution)/shard_map/all_to_all | solution.py:17
  120.1 6.8 %all_to_all.34 = f32[2,16,32,512]{3,2,1,0:T(8,128)S(1)} all-to-all(f32[2,16,32,512]{3,2,1,0:T(8,128)S(1)} %broadcast_in_dim.11), channel_id=1, replica_groups=mesh['fsdp'=8,'tensor_0'=4,'tensor_1'=4,'tensor_2'=2] {'tensor_2'}, dimensions={0} | all-to-all | bytes 4194304 | tf_op jit(solution)/shard_map/all_to_all | solution.py:17
  126.8 4.5 fusion.9
  135.5 162.9 %all-gather.3.cloned.1.call-done = f32[4096,512]{1,0:T(8,128)} async-done(((f32[512,512]{1,0:T(8,128)}), f32[4096,512]{1,0:T(8,128)}) %all-gather.3.cloned.1.call-update) | async-done | bytes 8388624 | tf_op jit(solution)/shard_map/all_gather | solution.py:89
  298.3 4.5 reduce_sum.47
  306.6 11.7 %cholesky.104 = f32[128,128]{1,0:T(8,128)S(1)} custom-call(f32[128,128]{1,0:T(8,128)S(1)} %cholesky.266), custom_call_target="Cholesky" | custom-call | tf_op jit(solution)/shard_map/jit(cholesky)/cholesky | solution.py:94
  318.5 9.8 %custom-call.31 = f32[1,128,128]{1,2,0:T(8,128)S(1)} custom-call(f32[1,128,128]{2,1,0:T(8,128)S(1)} %get-tuple-element.45), custom_call_target="InvertDiagBlocksLowerTriangular" | custom-call | tf_op jit(solution)/shard_map/jit(cholesky)/cholesky | solution.py:94
  330.8 11.9 %cholesky.217 = f32[128,128]{1,0:T(8,128)S(1)} custom-call(f32[128,128]{1,0:T(8,128)S(1)} %cholesky.270), custom_call_target="Cholesky" | custom-call | tf_op jit(solution)/shard_map/jit(cholesky)/cholesky | solution.py:94
  342.7 9.8 %custom-call.32 = f32[1,128,128]{1,2,0:T(8,128)S(1)} custom-call(f32[1,128,128]{2,1,0:T(8,128)S(1)} %get-tuple-element.42), custom_call_target="InvertDiagBlocksLowerTriangular" | custom-call | tf_op jit(solution)/shard_map/jit(cholesky)/cholesky | solution.py:94
  354.1 11.7 %cholesky.238 = f32[128,128]{1,0:T(8,128)S(1)} custom-call(f32[128,128]{1,0:T(8,128)S(1)} %cholesky.275), custom_call_target="Cholesky" | custom-call | tf_op jit(solution)/shard_map/jit(cholesky)/cholesky | solution.py:94
  366.6 9.8 %custom-call.33 = f32[1,128,128]{1,2,0:T(8,128)S(1)} custom-call(f32[1,128,128]{2,1,0:T(8,128)S(1)} %get-tuple-element.39), custom_call_target="InvertDiagBlocksLowerTriangular" | custom-call | tf_op jit(solution)/shard_map/jit(cholesky)/cholesky | solution.py:94
  377.8 11.9 %cholesky.255 = f32[128,128]{1,0:T(8,128)S(1)} custom-call(f32[128,128]{1,0:T(8,128)S(1)} %convolution_subtract_fusion.4), custom_call_target="Cholesky" | custom-call | tf_op jit(solution)/shard_map/jit(cholesky)/cholesky | solution.py:94
  394.7 14.1 %while.1 = (s32[]{:T(128)}, f32[512,512]{1,0:T(8,128)}, s32[4,2]{0,1:T(2,128)S(1)}, f32[4,128,128]{2,1,0:T(8,128)}, s32[]{:T(128)}) while((s32[]{:T(128)}, f32[512,512]{1,0:T(8,128)}, s32[4,2]{0,1:T(2,128)S(1)}, f32[4,128,128]{2,1,0:T(8,128)}, s32[]{:T(128)}) %tuple.39), condition=%wide.while_cond, body=%wide.while_body.sunk | while | flops 2 | bytes 132705 | solution.py:95
  402.5 2.9 bitcast_dynamic-update-slice_fusion.2
  408.8 40.1 %custom-call.34 = f32[4,128,128]{1,2,0:T(8,128)S(1)} custom-call(f32[4,128,128]{2,1,0:T(8,128)} %get-tuple-element.10), custom_call_target="InvertDiagBlocksLowerTriangular" | custom-call | tf_op jit(solution)/shard_map/jit(_solve_triangular)/triangular_solve | solution.py:95
  459.0 101.2 %all-reduce.3.cloned.1.call-done = bf16[896,512]{1,0:T(8,128)(2,1)} async-done(((bf16[896,512]{1,0:T(8,128)(2,1)}), bf16[896,512]{1,0:T(8,128)(2,1)}) %all-reduce.3.cloned.1.call-update) | async-done | bytes 917520 | tf_op jit(solution)/shard_map/psum | solution.py:100
  562.3 11.4 %all-to-all-start.5 = ((f32[32,1,512]{2,1,0:T(1,128)}), f32[32,1,512]{2,1,0:T(1,128)S(1)}, u32[]{:S(2)}, u32[]{:S(2)}) async-start(f32[32,1,512]{2,1,0:T(1,128)} %broadcast_in_dim.12), calls=%async_computation.5 | async-start | bytes 131072 | tf_op jit(solution)/shard_map/all_to_all | solution.py:17
  573.7 4.0 subtract_convert_fusion
  577.7 3.7 all-to-all-done.5
  (82 shorter events, 49.9 us)
Async XLA Ops:
  7.2 13.8 %copy-start.2 = (bf16[1024,896]{1,0:T(8,128)(2,1)S(1)}, bf16[1024,896]{1,0:T(8,128)(2,1)}, u32[]{:S(2)}) copy-start(bf16[1024,896]{1,0:T(8,128)(2,1)} %param.4) | copy-start | bytes 5505028
  9.3 27.9 %all-to-all-start = ((bf16[8,896,64]{1,2,0:T(8,128)(2,1)}), bf16[8,896,64]{1,2,0:T(8,128)(2,1)S(1)}, u32[]{:S(2)}, u32[]{:S(2)}) async-start(bf16[8,896,64]{1,2,0:T(8,128)(2,1)} %broadcast_in_dim.9), calls=%async_computation | async-start | bytes 1835008 | tf_op jit(solution)/shard_map/all_to_all | solution.py:17
  21.0 277.4 %all-gather.3.cloned.1.call-start = ((), (), s32[]{:S(2)}) async-start(), calls=%async_computation.7 | async-start | bytes 9437184 | tf_op jit(solution)/shard_map/all_gather | solution.py:89
  131.4 428.9 %all-reduce.3.cloned.1.call-start = ((), (), s32[]{:S(2)}) async-start(), calls=%async_computation.6 | async-start | bytes 1835008 | tf_op jit(solution)/shard_map/psum | solution.py:100
  305.6 1.0 copy-start.1
  451.6 5.2 copy-start.5
  454.0 2.8 copy-start.7
  454.0 2.8 copy-start.3
  456.9 116.8 %copy-start.4 = (bf16[1024,896]{1,0:T(8,128)(2,1)S(1)}, bf16[1024,896]{1,0:T(8,128)(2,1)}, u32[]{:S(2)}) copy-start(bf16[1024,896]{1,0:T(8,128)(2,1)} %add_convert_fusion) | copy-start | bytes 5505028
  562.3 19.0 %all-to-all-start.5 = ((f32[32,1,512]{2,1,0:T(1,128)}), f32[32,1,512]{2,1,0:T(1,128)S(1)}, u32[]{:S(2)}, u32[]{:S(2)}) async-start(f32[32,1,512]{2,1,0:T(1,128)} %broadcast_in_dim.12), calls=%async_computation.5 | async-start | bytes 131072 | tf_op jit(solution)/shard_map/all_to_all | solution.py:17
  573.7 7.7 %copy-start = (bf16[896,512]{1,0:T(8,128)(2,1)S(1)}, bf16[896,512]{1,0:T(8,128)(2,1)}, u32[]{:S(2)}) copy-start(bf16[896,512]{1,0:T(8,128)(2,1)} %all-reduce.3.cloned.1.call-done) | copy-start | bytes 2752516
  581.5 1.3 copy-start.6
  581.5 1.3 copy-start.8
Sparse Core Ops, SparseCore 0:
  131.5 166.8 all-gather.2
  459.1 101.0 all-reduce.2
